TPU v7x, 128 devices: a whole 4x4x4 slice. The times are simulated.
128 devices in a mesh: section: 16 (over z_hi, y, core), seq: 8 (over x, z_lo).
Axes of the slice: x: 4, y: 4, z: 4 (z_hi: 2, z_lo: 2; z = z_hi * 2 + z_lo), core: 2. Of those that a mesh axis runs over, the one named last changes fastest.
Arguments:
- stash_query: bfloat16 [16, 1, 1536, 8192], P('section', None, 'seq'), may hold values from -8 to 8
- stash_key: bfloat16 [16, 1, 1536, 1024], P('section', None, 'seq'), may hold values from -8 to 8
- stashed_value_inputs: bfloat16 [16, 1, 1536, 1024], P('section', None, 'seq'), may hold values from -6 to 6
- grad_out: bfloat16 [16, 1, 1536, 8192], P('section', None, 'seq'), may hold values from -6 to 6
- partner: int32 [16], replicated, may hold values from 0 to 15, as said below
- span_order: int32 [16], replicated, may hold values from 0 to 15, each once
Outputs:
- grad_query: bfloat16 [16, 1, 1536, 8192], P('section', None, 'seq')
- grad_key: bfloat16 [16, 1, 1536, 1024], P('section', None, 'seq')
- grad_value: bfloat16 [16, 1, 1536, 1024], P('section', None, 'seq')
Inputs may be any that keep to these rules, and one draw needn't show every extreme that they name: partner[s] = s XOR p for one p of 1 to 15, the same p for every s.
All inputs are finite; a program needn't handle non-finite values.
Results may differ from a plain program's by a relative error of at most 0.0045.
The roundings to bfloat16 on the way count: a program that leaves them out, or rounds other values in their place, can miss the bound.
Values may be sent and summed in bfloat16 or wider, within the bound.
A program may use at most 192 MiB of HBM per device.

v0:
```python
import math

import jax
import jax.numpy as jnp
from jax import lax
from jax.sharding import PartitionSpec as P

QUERY_HEADS = 64
KEY_VALUE_HEADS = 8
HEAD_SIZE = 128


def for_sending(x):
    return jax.tree.map(lambda a: a.astype(jnp.bfloat16) if a.dtype == jnp.float32 else a, x)


def partner_2(block, axis, stride):
    count = lax.axis_size(axis)
    route = []
    for low in range(count):
        high = low | 1 << stride
        if high != low and high < count:
            route += [(low, high), (high, low)]
    return lax.ppermute(block, axis, route)


def frequencies(head_width):
    return jnp.power(
        jnp.float32(1000000.0), -jnp.arange(0, head_width, 2).astype(jnp.float32) / head_width
    )


def apply_rotary_heads(vectors, token_index_list, orientation):
    half_width = vectors.shape[-1] // 2
    angles = token_index_list.astype(jnp.float32)[:, None] * frequencies(vectors.shape[-1])[None, :]
    cosine_table = jnp.cos(angles)[:, None, :]
    sine_table = jnp.sin(angles)[:, None, :]
    first_half = vectors[..., :half_width]
    second_half = vectors[..., half_width:]
    return jnp.concatenate(
        [
            first_half * cosine_table - orientation * second_half * sine_table,
            second_half * cosine_table + orientation * first_half * sine_table,
        ],
        axis=-1,
    )


def token_positions(order_table, row_index, span_rows):
    block_index = row_index // span_rows
    table_index = jnp.arange(order_table.shape[0], dtype=jnp.int32)
    picked = jnp.sum(
        jnp.where(block_index[:, None] == table_index[None, :], order_table[None, :], 0), axis=1
    )
    return picked * span_rows + row_index % span_rows


def attend(rotated_queries, rotated_keys, value_row_block, gradient_rows, query_pos, key_pos):
    query_count, head_count, head_width = rotated_queries.shape
    key_count = rotated_keys.shape[0]
    group_count = rotated_keys.shape[1]
    queries_per_group = head_count // group_count
    block_rows = math.gcd(query_count, 512)
    block_count = query_count // block_rows
    score_scale = head_width ** (-0.5)
    keys_here = rotated_keys[:, 0, :]
    values_here = value_row_block[:, 0, :]
    query_blocks = rotated_queries.reshape(block_count, block_rows, queries_per_group, head_width)
    grad_blocks = gradient_rows.reshape(block_count, block_rows, queries_per_group, head_width)
    pos_blocks = query_pos.reshape(block_count, block_rows)

    def block_step(carried, pieces):
        key_total, value_total = carried
        query_block, grad_block, pos_block = pieces
        scores = (
            jnp.einsum("qrd,kd->rqk", query_block, keys_here, preferred_element_type=jnp.float32)
            * score_scale
        )
        scores = jnp.where(key_pos[None, None, :] <= pos_block[None, :, None], scores, -jnp.inf)
        shifted = jnp.exp(scores - jnp.max(scores, axis=-1, keepdims=True))
        attention_weights = shifted / jnp.sum(shifted, axis=-1, keepdims=True)
        weights_low = attention_weights.astype(jnp.bfloat16)
        grad_weights = jnp.einsum(
            "qrd,kd->rqk", grad_block, values_here, preferred_element_type=jnp.float32
        )
        row_delta = jnp.sum(attention_weights * grad_weights, axis=-1, keepdims=True)
        grad_scores = (attention_weights * (grad_weights - row_delta)).astype(jnp.bfloat16)
        grad_query_rot = (
            jnp.einsum("rqk,kd->qrd", grad_scores, keys_here, preferred_element_type=jnp.float32)
            * score_scale
        )
        key_term = (
            jnp.einsum("rqk,qrd->kd", grad_scores, query_block, preferred_element_type=jnp.float32)
            * score_scale
        )
        value_term = jnp.einsum(
            "rqk,qrd->kd", weights_low, grad_block, preferred_element_type=jnp.float32
        )
        return ((key_total + key_term, value_total + value_term), grad_query_rot)

    zeros_start = jnp.zeros((key_count, head_width), jnp.float32)
    (key_total, value_total), query_grad = lax.scan(
        block_step, (zeros_start, zeros_start), (query_blocks, grad_blocks, pos_blocks)
    )
    query_parts = query_grad.reshape(query_count, queries_per_group, head_width)
    key_parts = [key_total]
    value_parts = [value_total]
    return (query_parts, jnp.stack(key_parts, axis=1), jnp.stack(value_parts, axis=1))


def fetch_all(stashed, mask_bits):
    for bit_index in range(lax.axis_size("section").bit_length() - 1):
        arrived = jax.tree.map(
            lambda part, own: part.astype(own.dtype),
            partner_2(for_sending(stashed), "section", bit_index),
            stashed,
        )
        taken = mask_bits // 2**bit_index % 2 == 1
        stashed = jax.tree.map(
            lambda current, incoming: jnp.where(taken, incoming, current), stashed, arrived
        )
    return stashed


def layer_grads(query, key_row_block, value_row_block, gradient_rows, section_positions, all_pos):
    token_rows = query.shape[0]
    rotated_queries = apply_rotary_heads(
        query.reshape(token_rows, QUERY_HEADS, HEAD_SIZE).astype(jnp.float32),
        section_positions,
        1.0,
    ).astype(jnp.bfloat16)
    rotated_keys = apply_rotary_heads(
        key_row_block.reshape(token_rows, KEY_VALUE_HEADS, HEAD_SIZE).astype(jnp.float32),
        section_positions,
        1.0,
    ).astype(jnp.bfloat16)
    moved = (
        lax.all_to_all(
            rotated_queries.reshape(token_rows, QUERY_HEADS * HEAD_SIZE),
            "seq",
            split_axis=1,
            concat_axis=0,
            tiled=True,
        ),
        lax.all_to_all(
            rotated_keys.reshape(token_rows, KEY_VALUE_HEADS * HEAD_SIZE),
            "seq",
            split_axis=1,
            concat_axis=0,
            tiled=True,
        ),
        lax.all_to_all(value_row_block, "seq", split_axis=1, concat_axis=0, tiled=True),
        lax.all_to_all(gradient_rows, "seq", split_axis=1, concat_axis=0, tiled=True),
    )
    total_rows = moved[0].shape[0]
    local_queries = moved[0].shape[1] // HEAD_SIZE
    local_keys = moved[1].shape[1] // HEAD_SIZE
    grad_query_rot, rotated_key_gradient, summed_value_gradient = attend(
        moved[0].reshape(total_rows, local_queries, HEAD_SIZE),
        moved[1].reshape(total_rows, local_keys, HEAD_SIZE),
        moved[2].reshape(total_rows, local_keys, HEAD_SIZE),
        moved[3].reshape(total_rows, local_queries, HEAD_SIZE),
        all_pos,
        all_pos,
    )
    query_out = (
        apply_rotary_heads(grad_query_rot, all_pos, -1.0)
        .astype(jnp.bfloat16)
        .reshape(total_rows, local_queries * HEAD_SIZE)
    )
    key_out = (
        apply_rotary_heads(rotated_key_gradient, all_pos, -1.0)
        .astype(jnp.bfloat16)
        .reshape(total_rows, local_keys * HEAD_SIZE)
    )
    value_out = summed_value_gradient.astype(jnp.bfloat16).reshape(
        total_rows, local_keys * HEAD_SIZE
    )
    returned = (
        lax.all_to_all(query_out, "seq", split_axis=0, concat_axis=1, tiled=True),
        lax.all_to_all(key_out, "seq", split_axis=0, concat_axis=1, tiled=True),
        lax.all_to_all(value_out, "seq", split_axis=0, concat_axis=1, tiled=True),
    )
    return (returned[0], returned[1], returned[2])


def body(stash_query, stash_key, stashed_value_inputs, grad_out, partner, span_order):
    token_rows = stash_query.shape[2]
    seq_count = lax.axis_size("seq")
    span_rows = token_rows // 2
    local_rows = lax.axis_index("seq") * token_rows + jnp.arange(token_rows, dtype=jnp.int32)
    section_positions = token_positions(span_order, local_rows, span_rows)
    all_pos = token_positions(
        span_order, jnp.arange(token_rows * seq_count, dtype=jnp.int32), span_rows
    )
    mask_bits = partner[0]
    fetched = fetch_all((stash_query[0], stash_key[0], stashed_value_inputs[0]), mask_bits)
    query_in = fetched[0][0]
    key_in = fetched[1][0]
    value_in = fetched[2][0]
    query_out, key_out, value_out = layer_grads(
        query_in, key_in, value_in, grad_out[0, 0], section_positions, all_pos
    )
    query_list = [query_out]
    key_list = [key_out]
    value_list = [value_out]
    return (jnp.stack(query_list)[None], jnp.stack(key_list)[None], jnp.stack(value_list)[None])


def solution(mesh):
    placed = (
        P("section", None, "seq", None),
        P("section", None, "seq", None),
        P("section", None, "seq", None),
        P("section", None, "seq", None),
        P(),
        P(),
    )
    return jax.shard_map(
        body,
        mesh=mesh,
        in_specs=placed,
        out_specs=(
            P("section", None, "seq", None),
            P("section", None, "seq", None),
            P("section", None, "seq", None),
        ),
        check_vma=False,
    )
```

profile of v0, /device:TPU:72, one launch (start us, length us, event | category | flops | bytes accessed | tf_op | source)
XLA Modules:
  0.0 775.1 jit_solution(15255893681373611253)
XLA Ops:
  10.6 68.7 %collective-permute-done.1 = bf16[1,192,8192]{2,1,0:T(8,128)(2,1)} collective-permute-done((bf16[1,192,8192]{2,1,0:T(8,128)(2,1)S(1)}, bf16[1,192,8192]{2,1,0:T(8,128)(2,1)}, u32[]{:S(2)}, u32[]{:S(2)}) %collective-permute-start.1) | collective-permute-done | bytes 3145760 | tf_op jit(solution)/shard_map/ppermute | solution.py:24
  87.1 73.8 %collective-permute-done.5 = bf16[1,192,1024]{2,1,0:T(8,128)(2,1)S(1)} collective-permute-done((bf16[1,192,1024]{2,1,0:T(8,128)(2,1)S(1)}, bf16[1,192,1024]{2,1,0:T(8,128)(2,1)S(1)}, u32[]{:S(2)}, u32[]{:S(2)}) %collective-permute-start.5) | collective-permute-done | bytes 393248 | tf_op jit(solution)/shard_map/ppermute | solution.py:24
  161.8 10.4 %collective-permute-done.6 = bf16[1,192,1024]{2,1,0:T(8,128)(2,1)} collective-permute-done((bf16[1,192,1024]{2,1,0:T(8,128)(2,1)S(1)}, bf16[1,192,1024]{2,1,0:T(8,128)(2,1)}, u32[]{:S(2)}, u32[]{:S(2)}) %collective-permute-start.6) | collective-permute-done | bytes 393248 | tf_op jit(solution)/shard_map/ppermute | solution.py:24
  201.5 52.0 %all-to-all-done.1 = bf16[192,8,128]{2,0,1:T(8,128)(2,1)S(1)} async-done(((bf16[192,8,128]{2,0,1:T(8,128)(2,1)}), bf16[192,8,128]{2,0,1:T(8,128)(2,1)S(1)}, u32[]{:S(2)}, u32[]{:S(2)}) %all-to-all-start.1) | async-done | bytes 393248 | tf_op jit(solution)/shard_map/all_to_all | solution.py:145
  278.9 22.7 %all-to-all-done.2 = bf16[192,8,1024]{2,0,1:T(8,128)(2,1)} async-done(((bf16[192,8,1024]{2,0,1:T(8,128)(2,1)}), bf16[192,8,1024]{2,0,1:T(8,128)(2,1)}, u32[]{:S(2)}, u32[]{:S(2)}) %all-to-all-start.2) | async-done | bytes 3145760 | tf_op jit(solution)/shard_map/all_to_all | solution.py:153
  308.7 10.5 %collective-permute-done.9 = bf16[1,192,1024]{2,1,0:T(8,128)(2,1)S(1)} collective-permute-done((bf16[1,192,1024]{2,1,0:T(8,128)(2,1)S(1)}, bf16[1,192,1024]{2,1,0:T(8,128)(2,1)S(1)}, u32[]{:S(2)}, u32[]{:S(2)}) %collective-permute-start.9) | collective-permute-done | bytes 393248 | tf_op jit(solution)/shard_map/ppermute | solution.py:24
  320.4 10.9 %collective-permute-done.10 = bf16[1,192,1024]{2,1,0:T(8,128)(2,1)S(1)} collective-permute-done((bf16[1,192,1024]{2,1,0:T(8,128)(2,1)S(1)}, bf16[1,192,1024]{2,1,0:T(8,128)(2,1)S(1)}, u32[]{:S(2)}, u32[]{:S(2)}) %collective-permute-start.10) | collective-permute-done | bytes 393248 | tf_op jit(solution)/shard_map/ppermute | solution.py:24
  332.0 16.7 %collective-permute-done.11 = bf16[1,192,1024]{2,1,0:T(8,128)(2,1)S(1)} collective-permute-done((bf16[1,192,1024]{2,1,0:T(8,128)(2,1)S(1)}, bf16[1,192,1024]{2,1,0:T(8,128)(2,1)S(1)}, u32[]{:S(2)}, u32[]{:S(2)}) %collective-permute-start.11) | collective-permute-done | bytes 393248 | tf_op jit(solution)/shard_map/ppermute | solution.py:24
  363.6 317.9 %while.15 = (s32[]{:T(128)}, f32[1536,128]{1,0:T(8,128)}, f32[1536,128]{1,0:T(8,128)}, f32[3,512,8,128]{3,2,1,0:T(8,128)}, s32[1536]{0:T(1024)S(1)}, /*index=5*/...) while((s32[]{:T(128)}, f32[1536,128]{1,0:T(8,128)}, ...), condition=%wide.region_6.7_spmd.clone, body=%wide.region_2.6_spmd.clone.sunk | while | flops 8149726720 | bytes 368816864 | solution.py:102
  379.4 10.2 %fusion.74 = f32[512,8,1536]{2,0,1:T(8,128)} fusion(bf16[1,512,8,128]{3,2,1,0:T(8,128)(2,1)S(1)} %get-tuple-element.253, bf16[1536,128]{1,0:T(8,128)(2,1)S(1)} %get-tuple-element.290), kind=kOutput, calls=%fused_computation.27.clone.1 | convolution fusion | flops 1610612736 | bytes 26607616 | tf_op jit(solution)/shard_map/while/body/eval_jaxpr/qrd,kd->rqk/dot_general | solution.py:76
  390.1 29.0 %fusion.75 = (f32[8,512]{1,0:T(8,128)S(1)}, f32[8,512,1536]{2,1,0:T(8,128)}) fusion(f32[512,8,1536]{2,0,1:T(8,128)} %fusion.74, pred[512,1536]{1,0:T(8,128)(4,1)S(1)} %broadcast_compare_fusion.2), kind=kOutput, calls=%fused_computation.106.clone.1 | output fusion | flops 37750272 | bytes 51134464 | tf_op jit(solution)/shard_map/while/body/eval_jaxpr/sub | solution.py:80
  419.1 16.4 %fusion.76 = (f32[8,512]{1,0:T(8,128)S(1)}, f32[512,8,1536]{2,0,1:T(8,128)}) fusion(f32[8,512,1536]{2,1,0:T(8,128)} %get-tuple-element.254, f32[8,512]{1,0:T(8,128)S(1)} %get-tuple-element.255, bf16[1536,128]{1,0:T(8,128)(2,1)} %get-tuple-element.292, bf16[1,512,8,128]{3,2,1,0:T(8,128)(2,1)S(1)} %get-tuple-element.256), kind=kOutput, calls=%fused_computation.3.clone.1 | convolution fusion | flops 1629483008 | bytes 51806208 | tf_op jit(solution)/shard_map/while/body/eval_jaxpr/qrd,kd->rqk/dot_general | solution.py:83
  435.4 16.3 %fusion.77 = bf16[8,512,1536]{2,1,0:T(8,128)(2,1)S(1)} fusion(f32[512,8,1536]{2,0,1:T(8,128)} %get-tuple-element.257, f32[8,512]{1,0:T(8,128)S(1)} %get-tuple-element.258, f32[8,512,1536]{2,1,0:T(8,128)} %get-tuple-element.254, f32[8,512]{1,0:T(8,128)S(1)} %get-tuple-element.255), kind=kLoop, calls=%fused_computation.5.clone.1 | loop fusion | flops 25165824 | bytes 62947328 | tf_op jit(solution)/shard_map/while/body/eval_jaxpr/convert_element_type | solution.py:87
  458.9 14.1 %fusion.79 = f32[1536,128]{1,0:T(8,128)} fusion(bf16[1,512,8,128]{3,2,1,0:T(8,128)(2,1)} %copy-done.3, f32[1536,128]{1,0:T(8,128)} %get-tuple-element.273, pred[]{:T(512)S(6)} %compare.14, f32[8,512,1536]{2,1,0:T(8,128)} %get-tuple-element.254, f32[8,512]{1,0:T(8,128)S(1)} %get-tuple-element.255), kind=kOutput, calls=%fused_computation.20.clone.1 | convolution fusion | flops 1623588864 | bytes 27803648 | tf_op jit(solution)/shard_map/while/body/eval_jaxpr/rqk,qrd->kd/dot_general | solution.py:96
  480.3 10.2 %fusion.74 = f32[512,8,1536]{2,0,1:T(8,128)} fusion(bf16[1,512,8,128]{3,2,1,0:T(8,128)(2,1)S(1)} %get-tuple-element.253, bf16[1536,128]{1,0:T(8,128)(2,1)S(1)} %get-tuple-element.290), kind=kOutput, calls=%fused_computation.27.clone.1 | convolution fusion | flops 1610612736 | bytes 26607616 | tf_op jit(solution)/shard_map/while/body/eval_jaxpr/qrd,kd->rqk/dot_general | solution.py:76
  491.0 29.0 %fusion.75 = (f32[8,512]{1,0:T(8,128)S(1)}, f32[8,512,1536]{2,1,0:T(8,128)}) fusion(f32[512,8,1536]{2,0,1:T(8,128)} %fusion.74, pred[512,1536]{1,0:T(8,128)(4,1)S(1)} %broadcast_compare_fusion.2), kind=kOutput, calls=%fused_computation.106.clone.1 | output fusion | flops 37750272 | bytes 51134464 | tf_op jit(solution)/shard_map/while/body/eval_jaxpr/sub | solution.py:80
  519.9 16.4 %fusion.76 = (f32[8,512]{1,0:T(8,128)S(1)}, f32[512,8,1536]{2,0,1:T(8,128)}) fusion(f32[8,512,1536]{2,1,0:T(8,128)} %get-tuple-element.254, f32[8,512]{1,0:T(8,128)S(1)} %get-tuple-element.255, bf16[1536,128]{1,0:T(8,128)(2,1)} %get-tuple-element.292, bf16[1,512,8,128]{3,2,1,0:T(8,128)(2,1)S(1)} %get-tuple-element.256), kind=kOutput, calls=%fused_computation.3.clone.1 | convolution fusion | flops 1629483008 | bytes 51806208 | tf_op jit(solution)/shard_map/while/body/eval_jaxpr/qrd,kd->rqk/dot_general | solution.py:83
  536.3 16.3 %fusion.77 = bf16[8,512,1536]{2,1,0:T(8,128)(2,1)S(1)} fusion(f32[512,8,1536]{2,0,1:T(8,128)} %get-tuple-element.257, f32[8,512]{1,0:T(8,128)S(1)} %get-tuple-element.258, f32[8,512,1536]{2,1,0:T(8,128)} %get-tuple-element.254, f32[8,512]{1,0:T(8,128)S(1)} %get-tuple-element.255), kind=kLoop, calls=%fused_computation.5.clone.1 | loop fusion | flops 25165824 | bytes 62947328 | tf_op jit(solution)/shard_map/while/body/eval_jaxpr/convert_element_type | solution.py:87
  559.8 14.3 %fusion.79 = f32[1536,128]{1,0:T(8,128)} fusion(bf16[1,512,8,128]{3,2,1,0:T(8,128)(2,1)} %copy-done.3, f32[1536,128]{1,0:T(8,128)} %get-tuple-element.273, pred[]{:T(512)S(6)} %compare.14, f32[8,512,1536]{2,1,0:T(8,128)} %get-tuple-element.254, f32[8,512]{1,0:T(8,128)S(1)} %get-tuple-element.255), kind=kOutput, calls=%fused_computation.20.clone.1 | convolution fusion | flops 1623588864 | bytes 27803648 | tf_op jit(solution)/shard_map/while/body/eval_jaxpr/rqk,qrd->kd/dot_general | solution.py:96
  592.3 29.0 %fusion.75 = (f32[8,512]{1,0:T(8,128)S(1)}, f32[8,512,1536]{2,1,0:T(8,128)}) fusion(f32[512,8,1536]{2,0,1:T(8,128)} %fusion.74, pred[512,1536]{1,0:T(8,128)(4,1)S(1)} %broadcast_compare_fusion.2), kind=kOutput, calls=%fused_computation.106.clone.1 | output fusion | flops 37750272 | bytes 51134464 | tf_op jit(solution)/shard_map/while/body/eval_jaxpr/sub | solution.py:80
  621.3 16.4 %fusion.76 = (f32[8,512]{1,0:T(8,128)S(1)}, f32[512,8,1536]{2,0,1:T(8,128)}) fusion(f32[8,512,1536]{2,1,0:T(8,128)} %get-tuple-element.254, f32[8,512]{1,0:T(8,128)S(1)} %get-tuple-element.255, bf16[1536,128]{1,0:T(8,128)(2,1)} %get-tuple-element.292, bf16[1,512,8,128]{3,2,1,0:T(8,128)(2,1)S(1)} %get-tuple-element.256), kind=kOutput, calls=%fused_computation.3.clone.1 | convolution fusion | flops 1629483008 | bytes 51806208 | tf_op jit(solution)/shard_map/while/body/eval_jaxpr/qrd,kd->rqk/dot_general | solution.py:83
  637.7 16.3 %fusion.77 = bf16[8,512,1536]{2,1,0:T(8,128)(2,1)S(1)} fusion(f32[512,8,1536]{2,0,1:T(8,128)} %get-tuple-element.257, f32[8,512]{1,0:T(8,128)S(1)} %get-tuple-element.258, f32[8,512,1536]{2,1,0:T(8,128)} %get-tuple-element.254, f32[8,512]{1,0:T(8,128)S(1)} %get-tuple-element.255), kind=kLoop, calls=%fused_computation.5.clone.1 | loop fusion | flops 25165824 | bytes 62947328 | tf_op jit(solution)/shard_map/while/body/eval_jaxpr/convert_element_type | solution.py:87
  661.1 14.3 %fusion.79 = f32[1536,128]{1,0:T(8,128)} fusion(bf16[1,512,8,128]{3,2,1,0:T(8,128)(2,1)} %copy-done.3, f32[1536,128]{1,0:T(8,128)} %get-tuple-element.273, pred[]{:T(512)S(6)} %compare.14, f32[8,512,1536]{2,1,0:T(8,128)} %get-tuple-element.254, f32[8,512]{1,0:T(8,128)S(1)} %get-tuple-element.255), kind=kOutput, calls=%fused_computation.20.clone.1 | convolution fusion | flops 1623588864 | bytes 27803648 | tf_op jit(solution)/shard_map/while/body/eval_jaxpr/rqk,qrd->kd/dot_general | solution.py:96
  728.1 37.4 %all-to-all-done.4 = bf16[8,192,1024]{2,1,0:T(8,128)(2,1)S(1)} async-done(((bf16[8,192,1024]{2,1,0:T(8,128)(2,1)}), bf16[8,192,1024]{2,1,0:T(8,128)(2,1)S(1)}, u32[]{:S(2)}, u32[]{:S(2)}) %all-to-all-start.4) | async-done | bytes 3145760 | tf_op jit(solution)/shard_map/all_to_all | solution.py:180
  (145 shorter events, 206.0 us)
Async XLA Ops:
  0.6 6.1 collective-permute-start
  9.0 75.0 %copy-start.7 = (bf16[1,1,192,1024]{3,2,1,0:T(8,128)(2,1)S(1)}, bf16[1,1,192,1024]{3,2,1,0:T(8,128)(2,1)}, u32[]{:S(2)}) copy-start(bf16[1,1,192,1024]{3,2,1,0:T(8,128)(2,1)} %param.9) | copy-start | bytes 1179652
  9.0 152.2 %copy-start.12 = (s32[16]{0:T(128)S(1)}, s32[16]{0:T(128)}, u32[]{:S(2)}) copy-start(s32[16]{0:T(128)} %param.13) | copy-start | bytes 196
  9.0 70.3 %collective-permute-start.1 = (bf16[1,192,8192]{2,1,0:T(8,128)(2,1)S(1)}, bf16[1,192,8192]{2,1,0:T(8,128)(2,1)}, u32[]{:S(2)}, u32[]{:S(2)}) collective-permute-start(bf16[1,192,8192]{2,1,0:T(8,128)(2,1)S(1)} %broadcast_select_fusion), channel_id=1, source_target_pairs={{0,16},{16,0},{8,24},{24,8},{32,48},{48,32},{40,56},{56,40},{64,80... | collective-permute-start | bytes 9437192 | tf_op jit(solution)/shard_map/ppermute | solution.py:24
  81.5 91.7 %collective-permute-start.2 = (bf16[1,192,8192]{2,1,0:T(8,128)(2,1)S(1)}, bf16[1,192,8192]{2,1,0:T(8,128)(2,1)}, u32[]{:S(2)}, u32[]{:S(2)}) collective-permute-start(bf16[1,192,8192]{2,1,0:T(8,128)(2,1)S(1)} %broadcast_select_fusion.1), channel_id=1, source_target_pairs={{0,32},{32,0},{8,40},{40,8},{16,48},{48,16},{24,56},{56,24},{64,96... | collective-permute-start | bytes 9437192 | tf_op jit(solution)/shard_map/ppermute | solution.py:24
  83.9 1.7 collective-permute-start.4
  85.7 75.3 %collective-permute-start.5 = (bf16[1,192,1024]{2,1,0:T(8,128)(2,1)S(1)}, bf16[1,192,1024]{2,1,0:T(8,128)(2,1)S(1)}, u32[]{:S(2)}, u32[]{:S(2)}) collective-permute-start(bf16[1,192,1024]{2,1,0:T(8,128)(2,1)S(1)} %broadcast_select_fusion.4), channel_id=1, source_target_pairs={{0,16},{16,0},{8,24},{24,8},{32,48},{48,32},{40,56},{56,40},{64,80... | collective-permute-start | bytes 1179656 | tf_op jit(solution)/shard_map/ppermute | solution.py:24
  161.0 11.1 %collective-permute-start.6 = (bf16[1,192,1024]{2,1,0:T(8,128)(2,1)S(1)}, bf16[1,192,1024]{2,1,0:T(8,128)(2,1)}, u32[]{:S(2)}, u32[]{:S(2)}) collective-permute-start(bf16[1,192,1024]{2,1,0:T(8,128)(2,1)S(1)} %broadcast_select_fusion.6), channel_id=1, source_target_pairs={{0,32},{32,0},{8,40},{40,8},{16,48},{48,16},{24,56},{56,24},{64,96... | collective-permute-start | bytes 1179656 | tf_op jit(solution)/shard_map/ppermute | solution.py:24
  173.2 13.7 %collective-permute-start.7 = (bf16[1,192,1024]{2,1,0:T(8,128)(2,1)S(1)}, bf16[1,192,1024]{2,1,0:T(8,128)(2,1)}, u32[]{:S(2)}, u32[]{:S(2)}) collective-permute-start(bf16[1,192,1024]{2,1,0:T(8,128)(2,1)S(1)} %broadcast_select_fusion.8), channel_id=1, source_target_pairs={{0,64},{64,0},{8,72},{72,8},{16,80},{80,16},{24,88},{88,24},{32,96... | collective-permute-start | bytes 1179656 | tf_op jit(solution)/shard_map/ppermute | solution.py:24
  177.2 81.1 %collective-permute-start.3 = (bf16[1,192,8192]{2,1,0:T(8,128)(2,1)}, bf16[1,192,8192]{2,1,0:T(8,128)(2,1)}, u32[]{:S(2)}, u32[]{:S(2)}) collective-permute-start(bf16[1,192,8192]{2,1,0:T(8,128)(2,1)} %broadcast_select_fusion.2), channel_id=1, source_target_pairs={{0,64},{64,0},{8,72},{72,8},{16,80},{80,16},{24,88},{88,24},{32,96... | collective-permute-start | bytes 9437192 | tf_op jit(solution)/shard_map/ppermute | solution.py:24
  188.7 64.8 %all-to-all-start.1 = ((bf16[192,8,128]{2,0,1:T(8,128)(2,1)}), bf16[192,8,128]{2,0,1:T(8,128)(2,1)S(1)}, u32[]{:S(2)}, u32[]{:S(2)}) async-start(bf16[192,8,128]{2,0,1:T(8,128)(2,1)} %pad_maximum_fusion.2), calls=%async_computation.1 | async-start | bytes 786432 | tf_op jit(solution)/shard_map/all_to_all | solution.py:145
  253.5 48.1 %all-to-all-start.2 = ((bf16[192,8,1024]{2,0,1:T(8,128)(2,1)}), bf16[192,8,1024]{2,0,1:T(8,128)(2,1)}, u32[]{:S(2)}, u32[]{:S(2)}) async-start(bf16[192,8,1024]{2,0,1:T(8,128)(2,1)} %copy.72), calls=%async_computation.2 | async-start | bytes 6291456 | tf_op jit(solution)/shard_map/all_to_all | solution.py:153
  301.6 48.1 %all-to-all-start = ((bf16[192,8,1024]{2,0,1:T(8,128)(2,1)}), bf16[192,8,1024]{2,0,1:T(8,128)(2,1)}, u32[]{:S(2)}, u32[]{:S(2)}) async-start(bf16[192,8,1024]{2,0,1:T(8,128)(2,1)} %copy.69), calls=%async_computation | async-start | bytes 6291456 | tf_op jit(solution)/shard_map/all_to_all | solution.py:138
  306.1 1.8 collective-permute-start.8
  308.0 11.2 %collective-permute-start.9 = (bf16[1,192,1024]{2,1,0:T(8,128)(2,1)S(1)}, bf16[1,192,1024]{2,1,0:T(8,128)(2,1)S(1)}, u32[]{:S(2)}, u32[]{:S(2)}) collective-permute-start(bf16[1,192,1024]{2,1,0:T(8,128)(2,1)S(1)} %broadcast_select_fusion.3), channel_id=1, source_target_pairs={{0,16},{16,0},{8,24},{24,8},{32,48},{48,32},{40,56},{56,40},{64,80... | collective-permute-start | bytes 1179656 | tf_op jit(solution)/shard_map/ppermute | solution.py:24
  319.3 12.0 %collective-permute-start.10 = (bf16[1,192,1024]{2,1,0:T(8,128)(2,1)S(1)}, bf16[1,192,1024]{2,1,0:T(8,128)(2,1)S(1)}, u32[]{:S(2)}, u32[]{:S(2)}) collective-permute-start(bf16[1,192,1024]{2,1,0:T(8,128)(2,1)S(1)} %broadcast_select_fusion.5), channel_id=1, source_target_pairs={{0,32},{32,0},{8,40},{40,8},{16,48},{48,16},{24,56},{56,24},{64,96... | collective-permute-start | bytes 1179656 | tf_op jit(solution)/shard_map/ppermute | solution.py:24
  331.3 17.4 %collective-permute-start.11 = (bf16[1,192,1024]{2,1,0:T(8,128)(2,1)S(1)}, bf16[1,192,1024]{2,1,0:T(8,128)(2,1)S(1)}, u32[]{:S(2)}, u32[]{:S(2)}) collective-permute-start(bf16[1,192,1024]{2,1,0:T(8,128)(2,1)S(1)} %broadcast_select_fusion.7), channel_id=1, source_target_pairs={{0,64},{64,0},{8,72},{72,8},{16,80},{80,16},{24,88},{88,24},{32,96... | collective-permute-start | bytes 1179656 | tf_op jit(solution)/shard_map/ppermute | solution.py:24
  349.8 13.8 %all-to-all-start.3 = ((bf16[192,8,128]{2,0,1:T(8,128)(2,1)}), bf16[192,8,128]{2,0,1:T(8,128)(2,1)}, u32[]{:S(2)}, u32[]{:S(2)}) async-start(bf16[192,8,128]{2,0,1:T(8,128)(2,1)} %copy.73), calls=%async_computation.3 | async-start | bytes 786432 | tf_op jit(solution)/shard_map/all_to_all | solution.py:152
  363.6 317.9 %copy-start.9 = (f32[1536]{0:T(1024)S(1)}, f32[1536]{0:T(1024)}, u32[]{:S(2)}) copy-start(f32[1536]{0:T(1024)} %get-tuple-element.181) | copy-start | bytes 18436
  363.6 317.9 %copy-start.11 = (f32[64]{0:T(128)S(1)}, f32[64]{0:T(128)}, u32[]{:S(2)}) copy-start(f32[64]{0:T(128)} %copy-done.10) | copy-start | bytes 772
  379.4 39.7 %copy-start.3 = (bf16[1,512,8,128]{3,2,1,0:T(8,128)(2,1)}, bf16[1,512,8,128]{3,2,1,0:T(8,128)(2,1)S(1)}, u32[]{:S(2)}) copy-start(bf16[1,512,8,128]{3,2,1,0:T(8,128)(2,1)S(1)} %get-tuple-element.256) | copy-start | bytes 3145732 | tf_op jit(solution)/shard_map/while
  687.9 13.7 %all-to-all-start.5 = ((bf16[8,192,128]{2,1,0:T(8,128)(2,1)}), bf16[8,192,128]{2,1,0:T(8,128)(2,1)S(1)}, u32[]{:S(2)}, u32[]{:S(2)}) async-start(bf16[8,192,128]{2,1,0:T(8,128)(2,1)} %pad_maximum_fusion.3), calls=%async_computation.5 | async-start | bytes 786432 | tf_op jit(solution)/shard_map/all_to_all | solution.py:181
  701.7 15.7 %all-to-all-start.6 = ((bf16[8,192,128]{2,1,0:T(8,128)(2,1)}), bf16[8,192,128]{2,1,0:T(8,128)(2,1)}, u32[]{:S(2)}, u32[]{:S(2)}) async-start(bf16[8,192,128]{2,1,0:T(8,128)(2,1)} %bitcast.16), calls=%async_computation.6 | async-start | bytes 786432 | tf_op jit(solution)/shard_map/all_to_all | solution.py:182
  717.4 48.0 %all-to-all-start.4 = ((bf16[8,192,1024]{2,1,0:T(8,128)(2,1)}), bf16[8,192,1024]{2,1,0:T(8,128)(2,1)S(1)}, u32[]{:S(2)}, u32[]{:S(2)}) async-start(bf16[8,192,1024]{2,1,0:T(8,128)(2,1)} %convert_element_type.80), calls=%async_computation.4 | async-start | bytes 6291456 | tf_op jit(solution)/shard_map/all_to_all | solution.py:180
  (17 other events, 242.7 us)
where the time goes:
time: 787 us; the launch traced here: 775 us
  waiting for transfers between devices  321 us (41%)
  other arithmetic  176 us (22%)
  matrix products  150 us (19%)
  local copies, waits for them, and re-layouts  64.8 us (8%)
  starting transfers between devices  45 us (6%)
  loops' own time  14.5 us (2%)
    ppermute x12, waiting for transfers between devices, partner_2(): return lax.ppermute(block, axis, route)  204 us
    sub x3, other arithmetic, block_step(): shifted = jnp.exp(scores - jnp.max(scores, axis=-1, keepdims=True))  86.9 us
    all_to_all x1, waiting for transfers between devices, layer_grads(): lax.all_to_all(rotated_keys.reshape(token_rows, KEY_VALUE_HEADS * HEAD_SI...  52 us
    dot_general x3, matrix products, block_step(): jnp.einsum('qrd,kd->rqk', grad_block, values_here, preferred_element_type...  49.1 us
    convert_element_type x3, other arithmetic, block_step(): (attention_weights * (grad_weights - row_delta)).astype(jnp.bfloat16)  48.9 us
    dot_general x3, matrix products, block_step(): jnp.einsum('rqk,qrd->kd', weights_low, grad_block, preferred_element_type...  42.8 us
    all_to_all x1, waiting for transfers between devices, layer_grads(): lax.all_to_all(query_out, 'seq', split_axis=0, concat_axis=1, tiled=True)  37.4 us
    dot_general x3, matrix products, block_step(): jnp.einsum('qrd,kd->rqk', query_block, keys_here, preferred_element_type=...  30.5 us
  transfers between devices with their start and end apart: 19, of which 15 were waited for; matrix products, arithmetic and copies ran while one was open for 9% of the time, Pallas kernels for 0%

commit v1 on v0

v1 whole, which is shorter than its diff:
```python
import functools
import math

import jax
import jax.numpy as jnp
import numpy as np
from jax import lax
from jax.experimental import pallas as pl
from jax.experimental.pallas import tpu as pltpu
from jax.sharding import PartitionSpec as P

QUERY_HEADS = 64
KEY_VALUE_HEADS = 8
HEAD_SIZE = 128
GROUP = QUERY_HEADS // KEY_VALUE_HEADS
BLOCK = 256
MESH = pl.DeviceIdType.MESH


def rotary_table(tokens):
    half = HEAD_SIZE // 2
    steps = np.arange(0, HEAD_SIZE, 2).astype(np.float32) / np.float32(HEAD_SIZE)
    frequency = np.power(np.float32(1000000.0), -steps).astype(np.float32)
    angles = np.arange(tokens, dtype=np.float32)[:, None] * frequency[None, :]
    angles = angles.astype(np.float64)
    table = np.concatenate([np.cos(angles), np.sin(angles)], axis=1).astype(np.float32)
    assert table.shape == (tokens, 2 * half)
    return table


def xor_static(index, mask):
    result = index
    bit = 1
    while bit <= mask:
        if mask & bit:
            low = lax.rem(lax.div(index, bit), 2)
            result = result + (1 - 2 * low) * bit
        bit *= 2
    return result


def wait_bytes(like, sem):
    pltpu.make_async_copy(like, like, sem).wait()


def gather_kernel(pair, seq, q_ref, k_ref, v_ref, g_ref, q_all, k_all, v_all, g_all, send, recv, own):
    section = lax.axis_index("section")
    me = lax.axis_index("seq")
    other = xor_static(section, pair)
    rows = q_ref.shape[0]
    barrier = pltpu.get_barrier_semaphore()
    for j in range(seq):
        to = lax.rem(me + j, seq)
        pl.semaphore_signal(
            barrier, inc=1, device_id={"section": other, "seq": to}, device_id_type=MESH
        )
        if j:
            pl.semaphore_signal(
                barrier, inc=1, device_id={"section": section, "seq": to}, device_id_type=MESH
            )
    pl.semaphore_wait(barrier, 2 * seq - 1)
    wide = q_ref.shape[1] // seq
    thin = k_ref.shape[1] // seq
    mine = pl.ds(pl.multiple_of(me * rows, rows), rows)

    def columns(to, width):
        return pl.ds(pl.multiple_of(to * width, width), width)

    def send_to(source, to, width, target, index, device):
        pltpu.make_async_remote_copy(
            src_ref=source.at[:, columns(to, width)],
            dst_ref=target.at[mine],
            send_sem=send.at[index],
            recv_sem=recv.at[index],
            device_id={"section": device, "seq": to},
            device_id_type=MESH,
        ).start()

    def step(j, carry):
        to = lax.rem(me + j, seq)
        send_to(k_ref, to, thin, k_all, 0, other)
        send_to(v_ref, to, thin, v_all, 1, other)
        return carry

    lax.fori_loop(0, seq, step, 0)

    def wide_step(j, carry):
        to = lax.rem(me + j, seq)
        send_to(q_ref, to, wide, q_all, 2, other)

        @pl.when(j > 0)
        def _():
            send_to(g_ref, to, wide, g_all, 3, section)

        return carry

    lax.fori_loop(0, seq, wide_step, 0)
    local = pltpu.make_async_copy(g_ref.at[:, columns(me, wide)], g_all.at[mine], own)
    local.start()
    local.wait()
    shared = pl.ds(0, rows * (seq - 1))
    for sem in (send, recv):
        wait_bytes(k_all, sem.at[0])
        wait_bytes(v_all, sem.at[1])
        wait_bytes(q_all, sem.at[2])
        wait_bytes(g_all.at[shared], sem.at[3])


def gather(pair, seq, q, k, v, g):
    rows = q.shape[0]
    any_spec = pl.BlockSpec(memory_space=pl.ANY)

    def full(a):
        return jax.ShapeDtypeStruct((rows * seq, a.shape[1] // seq), a.dtype)

    return pl.pallas_call(
        functools.partial(gather_kernel, pair, seq),
        out_shape=(full(q), full(k), full(v), full(g)),
        in_specs=[any_spec] * 4,
        out_specs=(any_spec,) * 4,
        scratch_shapes=[
            pltpu.SemaphoreType.DMA((4,)),
            pltpu.SemaphoreType.DMA((4,)),
            pltpu.SemaphoreType.DMA(()),
        ],
        compiler_params=pltpu.CompilerParams(collective_id=pair, has_side_effects=True),
        name=f"gather_{pair}",
    )(q, k, v, g)


def dot(a, b, dims):
    return lax.dot_general(a, b, (dims, ((), ())), preferred_element_type=jnp.float32)


def attend_kernel(
    seq,
    span,
    order,
    inverse,
    q_all,
    k_all,
    v_all,
    g_all,
    table,
    dq_out,
    dk_out,
    dv_out,
    cosine,
    sine,
    qs,
    ks,
    vs,
    gs,
    kt,
    dk,
    dv,
    scores,
    gains,
    dqs,
    dvs,
    parcels,
    parcel_k,
    parcel_v,
    send,
    recv,
    own,
):
    section = lax.axis_index("section")
    me = lax.axis_index("seq")
    spans = k_all.shape[0]
    tokens = spans * span
    rows = tokens // seq
    half = HEAD_SIZE // 2
    blocks = tokens // BLOCK
    scale = HEAD_SIZE**-0.5
    scale2 = scale * math.log2(math.e)
    barrier = pltpu.get_barrier_semaphore()
    for j in range(1, seq):
        pl.semaphore_signal(
            barrier,
            inc=1,
            device_id={"section": section, "seq": lax.rem(me + j, seq)},
            device_id_type=MESH,
        )
    pl.semaphore_wait(barrier, seq - 1)

    def turn(x, at, sign):
        return x * cosine[at] + sign * (pltpu.roll(x, half, 1) * sine[at])

    first = lax.broadcasted_iota(jnp.int32, (span, HEAD_SIZE), 1) < half
    for b in range(spans):
        at = pl.ds(b * span, span)
        both = table[at]
        swapped = pltpu.roll(both, half, 1)
        cosine[at] = jnp.where(first, both, swapped)
        sine[at] = jnp.where(first, -swapped, both)
        key = turn(k_all[inverse[b]].astype(jnp.float32), at, 1.0)
        ks[at] = key.astype(jnp.bfloat16)
        vs[at] = v_all[inverse[b]]
    kt[...] = ks[...].T
    dk[...] = jnp.zeros_like(dk)
    dv[...] = jnp.zeros_like(dv)
    diagonal = lax.broadcasted_iota(jnp.int32, (BLOCK, BLOCK), 0) <= lax.broadcasted_iota(
        jnp.int32, (BLOCK, BLOCK), 1
    )
    parts = BLOCK // 8

    def send_to(source, target, index, j):
        to = lax.rem(me + j, seq)
        pltpu.make_async_remote_copy(
            src_ref=source.at[pl.ds(pl.multiple_of(to * rows, rows), rows)],
            dst_ref=target,
            send_sem=send.at[index],
            recv_sem=recv.at[index],
            device_id={"section": section, "seq": to},
            device_id_type=MESH,
        ).start()

    def scatter(source, target, index):
        for j in range(1, seq):
            send_to(source, target, index, j)
        pltpu.make_async_copy(
            source.at[pl.ds(pl.multiple_of(me * rows, rows), rows)], target, own.at[index]
        ).start()

    def keep_rows(target, start, value):
        stop = start + value.shape[0]
        row = start
        while row < stop:
            b, low = row // span, row % span
            size = min(span - low, stop - row)
            target[b, pl.ds(low, size)] = value[row - start : row - start + size]
            row += size

    def head(h, carry):
        lanes = pl.ds(pl.multiple_of(h * HEAD_SIZE, HEAD_SIZE), HEAD_SIZE)
        for b in range(spans):
            at = pl.ds(b * span, span)
            query = turn(q_all[inverse[b], :, lanes].astype(jnp.float32), at, 1.0)
            qs[at] = query.astype(jnp.bfloat16)
            gs[at] = g_all[inverse[b], :, lanes]
        for i in range(blocks):
            at = pl.ds(i * BLOCK, BLOCK)
            qb = qs[at]
            gb = gs[at]
            top = None
            for c in range(i + 1):
                keys = pl.ds(c * BLOCK, BLOCK)
                s = dot(ks[keys], qb, ((1,), (1,)))
                if c == i:
                    s = jnp.where(diagonal, s, -jnp.inf)
                scores[keys] = s
                part = jnp.max(s.reshape(parts, 8, BLOCK), axis=0)
                top = part if top is None else jnp.maximum(top, part)
            top = jnp.max(top, axis=0, keepdims=True)
            total = jnp.zeros((8, BLOCK), jnp.float32)
            mixed = jnp.zeros((8, BLOCK), jnp.float32)
            for c in range(i + 1):
                keys = pl.ds(c * BLOCK, BLOCK)
                e = jnp.exp2((scores[keys] - top) * scale2)
                gain = dot(vs[keys], gb, ((1,), (1,)))
                scores[keys] = e
                gains[keys] = gain
                total = total + jnp.sum(e.reshape(parts, 8, BLOCK), axis=0)
                mixed = mixed + jnp.sum((e * gain).reshape(parts, 8, BLOCK), axis=0)
            inv = 1.0 / jnp.sum(total, axis=0, keepdims=True)
            delta = jnp.sum(mixed, axis=0, keepdims=True) * inv
            dqt = jnp.zeros((HEAD_SIZE, BLOCK), jnp.float32)
            for c in range(i + 1):
                keys = pl.ds(c * BLOCK, BLOCK)
                weight = scores[keys] * inv
                low = weight.astype(jnp.bfloat16)
                ds = (weight * (gains[keys] - delta)).astype(jnp.bfloat16)
                dv[keys] += dot(low, gb, ((1,), (0,)))
                dk[keys] += dot(ds, qb, ((1,), (0,)))
                dqt = dqt + dot(kt[:, keys], ds, ((1,), (0,)))
            keep_rows(dqs, i * BLOCK, turn(dqt.T * scale, at, -1.0).astype(jnp.bfloat16))
        parcel = parcels.at[h]
        for b in range(spans):
            parcel[pl.ds(b * span, span)] = dqs[order[b]]
        column = pl.multiple_of((me * GROUP + h) * HEAD_SIZE, HEAD_SIZE)
        scatter(parcel, dq_out.at[:, pl.ds(column, HEAD_SIZE)], 0)
        return carry

    lax.fori_loop(0, GROUP, head, 0)
    for b in range(spans):
        at = pl.ds(b * span, span)
        dqs[b] = turn(dk[at] * scale, at, -1.0).astype(jnp.bfloat16)
        dvs[b] = dv[at].astype(jnp.bfloat16)
    for b in range(spans):
        parcel_k[pl.ds(b * span, span)] = dqs[order[b]]
        parcel_v[pl.ds(b * span, span)] = dvs[order[b]]
    column = pl.ds(pl.multiple_of(me * HEAD_SIZE, HEAD_SIZE), HEAD_SIZE)
    scatter(parcel_k, dk_out.at[:, column], 1)
    scatter(parcel_v, dv_out.at[:, column], 2)
    away = HEAD_SIZE * (seq - 1)
    for sem in (send, recv):
        wait_bytes(dq_out.at[:, pl.ds(0, GROUP * away)], sem.at[0])
        wait_bytes(dk_out.at[:, pl.ds(0, away)], sem.at[1])
        wait_bytes(dv_out.at[:, pl.ds(0, away)], sem.at[2])
    wait_bytes(dq_out.at[:, pl.ds(0, GROUP * HEAD_SIZE)], own.at[0])
    wait_bytes(dk_out.at[:, pl.ds(0, HEAD_SIZE)], own.at[1])
    wait_bytes(dv_out.at[:, pl.ds(0, HEAD_SIZE)], own.at[2])


def attend(seq, order, inverse, q_all, k_all, v_all, g_all):
    tokens = k_all.shape[0]
    rows = tokens // seq
    span = tokens // order.shape[0]
    smem = pl.BlockSpec(memory_space=pltpu.SMEM)
    vmem = pl.BlockSpec(memory_space=pltpu.VMEM)
    hbm = pl.BlockSpec(memory_space=pl.ANY)
    table = jnp.asarray(rotary_table(tokens))
    low = jnp.bfloat16
    thin = (tokens, HEAD_SIZE)
    tall = (tokens, BLOCK)
    return pl.pallas_call(
        functools.partial(attend_kernel, seq, span),
        out_shape=(
            jax.ShapeDtypeStruct((rows, seq * q_all.shape[1]), low),
            jax.ShapeDtypeStruct((rows, seq * HEAD_SIZE), low),
            jax.ShapeDtypeStruct((rows, seq * HEAD_SIZE), low),
        ),
        in_specs=[smem, smem] + [vmem] * 5,
        out_specs=(hbm,) * 3,
        scratch_shapes=[
            pltpu.VMEM(thin, jnp.float32),
            pltpu.VMEM(thin, jnp.float32),
            pltpu.VMEM(thin, low),
            pltpu.VMEM(thin, low),
            pltpu.VMEM(thin, low),
            pltpu.VMEM(thin, low),
            pltpu.VMEM((HEAD_SIZE, tokens), low),
            pltpu.VMEM(thin, jnp.float32),
            pltpu.VMEM(thin, jnp.float32),
            pltpu.VMEM(tall, jnp.float32),
            pltpu.VMEM(tall, jnp.float32),
            pltpu.VMEM((tokens // span, span, HEAD_SIZE), low),
            pltpu.VMEM((tokens // span, span, HEAD_SIZE), low),
            pltpu.VMEM((GROUP,) + thin, low),
            pltpu.VMEM(thin, low),
            pltpu.VMEM(thin, low),
            pltpu.SemaphoreType.DMA((3,)),
            pltpu.SemaphoreType.DMA((3,)),
            pltpu.SemaphoreType.DMA((3,)),
        ],
        compiler_params=pltpu.CompilerParams(
            collective_id=0, has_side_effects=True, vmem_limit_bytes=56 << 20
        ),
        name="attend",
    )(order, inverse, *(a.reshape(-1, span, a.shape[1]) for a in (q_all, k_all, v_all, g_all)), table)


def body(sections, seq, q, k, v, g, partner, order):
    span_index = jnp.arange(order.shape[0], dtype=jnp.int32)
    inverse = jnp.sum(
        jnp.where(order[:, None] == span_index[None, :], span_index[:, None], 0), axis=0
    )
    branches = [functools.partial(gather, pair, seq) for pair in range(1, sections)]
    moved = lax.switch(partner[0] - 1, branches, q[0, 0], k[0, 0], v[0, 0], g[0, 0])
    results = attend(seq, order, inverse, *moved)
    return tuple(result[None, None] for result in results)


def solution(mesh):
    placed = P("section", None, "seq", None)
    return jax.shard_map(
        functools.partial(body, mesh.shape["section"], mesh.shape["seq"]),
        mesh=mesh,
        in_specs=(placed, placed, placed, placed, P(), P()),
        out_specs=(placed, placed, placed),
        check_vma=False,
    )
```

time: 787 us -> 195 us (0.25); the launches traced: 775 us -> 193 us
  waiting for transfers between devices: 321 us -> 0 us
  Pallas kernels: 0 us -> 186 us
  other arithmetic: 176 us -> 0.6 us
  matrix products: 150 us -> 0 us
  local copies, waits for them, and re-layouts: 64.8 us -> 5.43 us
  starting transfers between devices: 45 us -> 0 us
  loops' own time: 14.5 us -> 0.05 us
    ppermute x12 -> x0, waiting for transfers between devices: 204 us -> none  [partner_2(): return lax.ppermute(block, axis, route)]
    pallas_call x0 -> x2, Pallas kernels: none -> 186 us  [the longest x1 108 us: gather(): pl.pallas_call(functools.partial(gather_kernel, pair, seq), out_shape=(fu...]
    dot_general x15 -> x0, matrix products: 150 us -> none  [the longest x3 49.1 us: block_step(): jnp.einsum('qrd,kd->rqk', grad_block, values_here, preferred_element_type...]
    all_to_all x7 -> x0, waiting for transfers between devices: 117 us -> none  [the longest x1 52 us: layer_grads(): lax.all_to_all(rotated_keys.reshape(token_rows, KEY_VALUE_HEADS * HEAD_SI...]
    sub x3 -> x0, other arithmetic: 86.9 us -> none  [block_step(): shifted = jnp.exp(scores - jnp.max(scores, axis=-1, keepdims=True))]
    convert_element_type x6 -> x0, other arithmetic: 50.4 us -> none  [the longest x3 48.9 us: block_step(): (attention_weights * (grad_weights - row_delta)).astype(jnp.bfloat16)]
    all_to_all x7 -> x0, starting transfers between devices: 34.4 us -> none  [the longest x1 5.75 us: layer_grads(): lax.all_to_all(key_out, 'seq', split_axis=0, concat_axis=1, tiled=True)]
    another operation x4 -> x0, other arithmetic: 15 us -> none
  transfers between devices with their start and end apart: 19 -> 0, of which waited for: 15 -> 0; matrix products, arithmetic and copies ran while one was open for 9% -> 0% of each run, Pallas kernels for 0% -> 0%
where the time goes in v1:
time: 195 us; the launch traced here: 193 us
  Pallas kernels  186 us (95%)
  local copies, waits for them, and re-layouts  5.43 us (3%)
    pallas_call x1, Pallas kernels, gather(): pl.pallas_call(functools.partial(gather_kernel, pair, seq), out_shape=(fu...  108 us
    pallas_call x1, Pallas kernels, attend(): pl.pallas_call(functools.partial(attend_kernel, seq, span), out_shape=(ja...  77.6 us
    unnamed x9, local copies, waits for them, and re-layouts  5.43 us

profile of v1, /device:TPU:72, one launch (start us, length us, event | category | flops | bytes accessed | tf_op | source)
XLA Modules:
  0.0 193.2 jit_solution(6818674909741215990)
XLA Ops:
  1.3 0.0 copy-start.2
  1.3 108.3 %conditional.1 = (bf16[16,96,1024]{2,1,0:T(8,128)(2,1)S(1)}, bf16[16,96,128]{2,1,0:T(8,128)(2,1)S(1)}, bf16[16,96,128]{2,1,0:T(8,128)(2,1)}, bf16[16,96,1024]{2,1,0:T(8,128)(2,1)}) conditional(s32[]{:T(128)} %bitcast.60, (bf16[192,8192]{1,0:T(8,128)(2,1)}, bf16[192,1024]{1,0:T(8,128)(2,1)}, ...), branch_computations={%region_1.2_spmd, %region_2.3_spmd, %region_3.4_spmd, %region_4.5_... | conditional | bytes 32 | solution.py:360
  1.3 108.3 %gather_1.1 = (bf16[1536,1024]{1,0:T(8,128)(2,1)S(1)}, bf16[1536,128]{1,0:T(8,128)(2,1)S(1)}, bf16[1536,128]{1,0:T(8,128)(2,1)}, bf16[1536,1024]{1,0:T(8,128)(2,1)}) custom-call(bf16[192,8192]{1,0:T(8,128)(2,1)} %get-tuple-element.184.q_ref, bf16[192,1024]{1,0:T(8,128)(2,1)} %get-tuple-element.185.k_ref, bf16[192,1024]{1,0:T(8,128)(2,1)} %get-tuple-element.186.v_ref, ...), custom_call_target="tpu_custom_call" | custom-call | tf_op jit(solution)/shard_map/cond/branch_0_fun/gather_1/pallas_call | solution.py:116
  109.6 0.0 copy-done.2
  109.6 0.6 select_reduce_fusion.inverse
  110.2 77.6 %attend.1 = (bf16[192,8192]{1,0:T(8,128)(2,1)}, bf16[192,1024]{1,0:T(8,128)(2,1)}, bf16[192,1024]{1,0:T(8,128)(2,1)}) custom-call(s32[16]{0:T(128)} %order.1, s32[16]{0:T(128)} %select_reduce_fusion.inverse, bf16[16,96,1024]{2,1,0:T(8,128)(2,1)S(1)} %get-tuple-element.314.q_all, bf16[16,96,128]{2,1,0:T(8,128)(2,1)S(1)} %get-tuple-element.315.k_all, ...), custom_call_target="tpu_custom_call" | custom-call | tf_op jit(solution)/shard_map/attend/pallas_call | solution.py:317
  187.8 0.0 copy-start.1
  187.8 0.0 copy-start
  187.8 3.9 %copy.73 = bf16[1,1,192,8192]{3,2,1,0:T(8,128)(2,1)} copy(bf16[1,1,192,8192]{3,2,1,0:T(8,128)(2,1)} %bitcast.129) | data formatting | bytes 6291456
  191.7 0.0 copy-done.1
  191.7 0.7 copy.74
  192.5 0.0 copy-done
  192.5 0.7 copy.75
Async XLA Ops:
  1.3 108.3 %copy-start.2 = (s32[16]{0:T(128)S(1)}, s32[16]{0:T(128)}, u32[]{:S(2)}) copy-start(s32[16]{0:T(128)} %order.1) | copy-start | bytes 196
  187.8 4.0 %copy-start.1 = (bf16[192,1024]{1,0:T(8,128)(2,1)S(1)}, bf16[192,1024]{1,0:T(8,128)(2,1)}, u32[]{:S(2)}) copy-start(bf16[192,1024]{1,0:T(8,128)(2,1)} %get-tuple-element.319) | copy-start | bytes 1179652
  187.8 4.7 %copy-start = (bf16[192,1024]{1,0:T(8,128)(2,1)S(1)}, bf16[192,1024]{1,0:T(8,128)(2,1)}, u32[]{:S(2)}) copy-start(bf16[192,1024]{1,0:T(8,128)(2,1)} %get-tuple-element.320) | copy-start | bytes 1179652

commit v2 on v1

v2 whole, which is shorter than its diff:
```python
import functools
import math

import jax
import jax.numpy as jnp
import numpy as np
from jax import lax
from jax.experimental import pallas as pl
from jax.experimental.pallas import tpu as pltpu
from jax.sharding import PartitionSpec as P

QUERY_HEADS = 64
KEY_VALUE_HEADS = 8
HEAD_SIZE = 128
GROUP = QUERY_HEADS // KEY_VALUE_HEADS
BLOCK = 256
CHUNK = 128
UNIT = 1
MESH = pl.DeviceIdType.MESH
MIXED = ((1, 0), (3, 0), (0, 1), (2, 0), (1, 1), (3, 1), (2, 1), (0, 0))


def rotary_table(tokens):
    half = HEAD_SIZE // 2
    steps = np.arange(0, HEAD_SIZE, 2).astype(np.float32) / np.float32(HEAD_SIZE)
    frequency = np.power(np.float32(1000000.0), -steps).astype(np.float32)
    angles = np.arange(tokens, dtype=np.float32)[:, None] * frequency[None, :]
    angles = angles.astype(np.float64)
    table = np.concatenate([np.cos(angles), np.sin(angles)], axis=1).astype(np.float32)
    assert table.shape == (tokens, 2 * half)
    return table


def xor_static(index, mask):
    result = index
    bit = 1
    while bit <= mask:
        if mask & bit:
            low = lax.rem(lax.div(index, bit), 2)
            result = result + (1 - 2 * low) * bit
        bit *= 2
    return result


def wait_bytes(like, sem):
    pltpu.make_async_copy(like, like, sem).wait()


def wait_own(like, sem):
    pltpu.make_async_copy(like, like, sem).wait()


def peer(me, seq, dx, dz):
    lines = seq // 2
    return lax.rem(lax.div(me, 2) + dx, lines) * 2 + lax.rem(lax.rem(me, 2) + dz, 2)


def gather_kernel(pair, seq, q_ref, k_ref, v_ref, g_ref, q_all, k_all, v_all, g_all, send, recv, own):
    section = lax.axis_index("section")
    me = lax.axis_index("seq")
    other = xor_static(section, pair)
    rows = q_ref.shape[0]
    targets = [(peer(me, seq, dx, dz), dx or dz) for dx, dz in MIXED]
    barrier = pltpu.get_barrier_semaphore()
    for to, away in targets:
        pl.semaphore_signal(
            barrier, inc=1, device_id={"section": other, "seq": to}, device_id_type=MESH
        )
        if away:
            pl.semaphore_signal(
                barrier, inc=1, device_id={"section": section, "seq": to}, device_id_type=MESH
            )
    pl.semaphore_wait(barrier, 2 * seq - 1)
    mine = pl.ds(pl.multiple_of(me * rows, rows), rows)

    def column(block):
        return pl.ds(pl.multiple_of(block * HEAD_SIZE, HEAD_SIZE), HEAD_SIZE)

    def send_to(source, to, target, index, device):
        pltpu.make_async_remote_copy(
            src_ref=source,
            dst_ref=target,
            send_sem=send.at[index],
            recv_sem=recv.at[index],
            device_id={"section": device, "seq": to},
            device_id_type=MESH,
        ).start()

    def step(h, carry):
        for to, away in targets:
            wide = column(to * GROUP + h)
            send_to(q_ref.at[:, wide], to, q_all.at[h, mine], 2, other)
            if away:
                send_to(g_ref.at[:, wide], to, g_all.at[h, mine], 3, section)
        pltpu.make_async_copy(
            g_ref.at[:, column(me * GROUP + h)], g_all.at[h, mine], own
        ).start()
        return carry

    for to, _ in targets:
        send_to(k_ref.at[:, column(to)], to, k_all.at[mine], 0, other)
        send_to(v_ref.at[:, column(to)], to, v_all.at[mine], 1, other)
    lax.fori_loop(0, GROUP, step, 0)
    wait_own(g_all.at[:, pl.ds(0, rows)], own)
    shared = pl.ds(0, rows * (seq - 1))
    for sem in (send, recv):
        wait_bytes(k_all, sem.at[0])
        wait_bytes(v_all, sem.at[1])
        wait_bytes(q_all, sem.at[2])
        wait_bytes(g_all.at[:, shared], sem.at[3])


def gather(pair, seq, q, k, v, g):
    rows = q.shape[0]
    any_spec = pl.BlockSpec(memory_space=pl.ANY)
    thin = jax.ShapeDtypeStruct((rows * seq, HEAD_SIZE), q.dtype)
    wide = jax.ShapeDtypeStruct((GROUP, rows * seq, HEAD_SIZE), q.dtype)
    return pl.pallas_call(
        functools.partial(gather_kernel, pair, seq),
        out_shape=(wide, thin, thin, wide),
        in_specs=[any_spec] * 4,
        out_specs=(any_spec,) * 4,
        scratch_shapes=[
            pltpu.SemaphoreType.DMA((4,)),
            pltpu.SemaphoreType.DMA((4,)),
            pltpu.SemaphoreType.DMA(()),
        ],
        compiler_params=pltpu.CompilerParams(collective_id=pair, has_side_effects=True, vmem_limit_bytes=2 << 20),
        name=f"gather_{pair}",
    )(q, k, v, g)


def dot(a, b, dims):
    return lax.dot_general(a, b, (dims, ((), ())), preferred_element_type=jnp.float32)


def attend_kernel(
    seq,
    span,
    order,
    inverse,
    q_all,
    k_all,
    v_all,
    g_all,
    table,
    dq_out,
    dk_out,
    dv_out,
    cosine,
    sine,
    qs,
    ks,
    vs,
    gs,
    kt,
    dk,
    dv,
    scores,
    gains,
    dqs,
    dvs,
    parcels,
    parcel_k,
    parcel_v,
    send,
    recv,
    own,
):
    section = lax.axis_index("section")
    me = lax.axis_index("seq")
    spans = k_all.shape[0]
    tokens = spans * span
    rows = tokens // seq
    half = HEAD_SIZE // 2
    blocks = tokens // BLOCK
    scale = HEAD_SIZE**-0.5
    scale2 = scale * math.log2(math.e)
    barrier = pltpu.get_barrier_semaphore()
    for j in range(1, seq):
        pl.semaphore_signal(
            barrier,
            inc=1,
            device_id={"section": section, "seq": lax.rem(me + j, seq)},
            device_id_type=MESH,
        )
    pl.semaphore_wait(barrier, seq - 1)

    def turn(x, at, sign):
        return x * cosine[at] + sign * (pltpu.roll(x, half, 1) * sine[at])

    first = lax.broadcasted_iota(jnp.int32, (span, HEAD_SIZE), 1) < half
    for b in range(spans):
        at = pl.ds(b * span, span)
        both = table[at]
        swapped = pltpu.roll(both, half, 1)
        cosine[at] = jnp.where(first, both, swapped)
        sine[at] = jnp.where(first, -swapped, both)
        key = turn(k_all[inverse[b]].astype(jnp.float32), at, 1.0)
        ks[at] = key.astype(jnp.bfloat16)
        vs[at] = v_all[inverse[b]]
    kt[...] = ks[...].T
    dk[...] = jnp.zeros_like(dk)
    dv[...] = jnp.zeros_like(dv)
    diagonal = lax.broadcasted_iota(jnp.int32, (BLOCK, BLOCK), 0) <= lax.broadcasted_iota(
        jnp.int32, (BLOCK, BLOCK), 1
    )
    parts = BLOCK // 8

    def send_to(source, target, index, to):
        pltpu.make_async_remote_copy(
            src_ref=source.at[pl.ds(pl.multiple_of(to * rows, rows), rows)],
            dst_ref=target,
            send_sem=send.at[index],
            recv_sem=recv.at[index],
            device_id={"section": section, "seq": to},
            device_id_type=MESH,
        ).start()

    def scatter(source, target, index):
        for dx, dz in MIXED:
            if dx or dz:
                send_to(source, target, index, peer(me, seq, dx, dz))
        pltpu.make_async_copy(
            source.at[pl.ds(pl.multiple_of(me * rows, rows), rows)], target, own.at[index]
        ).start()

    def keep_rows(target, start, value):
        stop = start + value.shape[0]
        row = start
        while row < stop:
            b, low = row // span, row % span
            size = min(span - low, stop - row)
            target[b, pl.ds(low, size)] = value[row - start : row - start + size]
            row += size

    def group(step, carry):
        for u in range(UNIT):
            h = step * UNIT + u
            for b in range(spans):
                at = pl.ds(b * span, span)
                query = turn(q_all[h, inverse[b]].astype(jnp.float32), at, 1.0)
                qs[u, at] = query.astype(jnp.bfloat16)
                gs[u, at] = g_all[h, inverse[b]]

        def start(u, i):
            score, gain_keep = scores.at[i % 2, u], gains.at[i % 2, u]
            qb = qs[u, pl.ds(i * BLOCK, BLOCK)]
            gb = gs[u, pl.ds(i * BLOCK, BLOCK)]
            tops = []
            top = None
            for c in range((i + 1) * BLOCK // CHUNK):
                keys = pl.ds(c * CHUNK, CHUNK)
                s = dot(ks[keys], qb, ((1,), (1,)))
                low_key = c * CHUNK - i * BLOCK
                if low_key >= 0:
                    s = jnp.where(diagonal[low_key : low_key + CHUNK], s, -jnp.inf)
                gain = dot(vs[keys], gb, ((1,), (1,)))
                part = jnp.max(jnp.max(s.reshape(CHUNK // 8, 8, BLOCK), axis=0), axis=0, keepdims=True)
                new = part if top is None else jnp.maximum(top, part)
                e = jnp.exp2((s - new) * scale2)
                score[keys] = e
                gain_keep[keys] = gain
                tsum = jnp.sum(e.reshape(CHUNK // 8, 8, BLOCK), axis=0)
                msum = jnp.sum((e * gain).reshape(CHUNK // 8, 8, BLOCK), axis=0)
                if top is None:
                    total, mixed = tsum, msum
                else:
                    fade = jnp.exp2((top - new) * scale2)
                    total = total * fade + tsum
                    mixed = mixed * fade + msum
                top = new
                tops.append(new)
            inv = 1.0 / jnp.sum(total, axis=0, keepdims=True)
            delta = jnp.sum(mixed, axis=0, keepdims=True) * inv
            return [inv * jnp.exp2((t - top) * scale2) for t in tops], delta

        def finish(i, ready):
            at = pl.ds(i * BLOCK, BLOCK)
            qb = jnp.concatenate([qs[u, at] for u in range(UNIT)], axis=0)
            gb = jnp.concatenate([gs[u, at] for u in range(UNIT)], axis=0)
            dqt = [jnp.zeros((HEAD_SIZE, BLOCK), jnp.float32)] * UNIT
            for c in range(i + 1):
                keys = pl.ds(c * BLOCK, BLOCK)
                wide_low, wide_ds = [], []
                for u in range(UNIT):
                    invs, delta = ready[u]
                    lows, dss = [], []
                    for f in range(BLOCK // CHUNK):
                        sub = pl.ds(c * BLOCK + f * CHUNK, CHUNK)
                        weight = scores[i % 2, u, sub] * invs[c * (BLOCK // CHUNK) + f]
                        lows.append(weight.astype(jnp.bfloat16))
                        dss.append((weight * (gains[i % 2, u, sub] - delta)).astype(jnp.bfloat16))
                    wide_low.append(jnp.concatenate(lows, axis=0))
                    ds = jnp.concatenate(dss, axis=0)
                    wide_ds.append(ds)
                    dqt[u] = dqt[u] + dot(kt[:, keys], ds, ((1,), (0,)))
                dv[keys] += dot(jnp.concatenate(wide_low, axis=1), gb, ((1,), (0,)))
                dk[keys] += dot(jnp.concatenate(wide_ds, axis=1), qb, ((1,), (0,)))
            for u in range(UNIT):
                keep_rows(dqs.at[u], i * BLOCK, turn(dqt[u].T * scale, at, -1.0).astype(jnp.bfloat16))

        ready = [start(u, 0) for u in range(UNIT)]
        for i in range(blocks):
            now = ready
            if i + 1 < blocks:
                ready = [start(u, i + 1) for u in range(UNIT)]
            finish(i, now)
        for u in range(UNIT):
            h = step * UNIT + u
            parcel = parcels.at[h]
            for b in range(spans):
                parcel[pl.ds(b * span, span)] = dqs[u, order[b]]
            column = pl.multiple_of((me * GROUP + h) * HEAD_SIZE, HEAD_SIZE)
            scatter(parcel, dq_out.at[:, pl.ds(column, HEAD_SIZE)], 0)
        return carry

    lax.fori_loop(0, GROUP // UNIT, group, 0)
    for b in range(spans):
        at = pl.ds(b * span, span)
        dqs[0, b] = turn(dk[at] * scale, at, -1.0).astype(jnp.bfloat16)
        dvs[b] = dv[at].astype(jnp.bfloat16)
    for b in range(spans):
        parcel_k[pl.ds(b * span, span)] = dqs[0, order[b]]
        parcel_v[pl.ds(b * span, span)] = dvs[order[b]]
    column = pl.ds(pl.multiple_of(me * HEAD_SIZE, HEAD_SIZE), HEAD_SIZE)
    scatter(parcel_k, dk_out.at[:, column], 1)
    scatter(parcel_v, dv_out.at[:, column], 2)
    away = HEAD_SIZE * (seq - 1)
    for sem in (send, recv):
        wait_bytes(dq_out.at[:, pl.ds(0, GROUP * away)], sem.at[0])
        wait_bytes(dk_out.at[:, pl.ds(0, away)], sem.at[1])
        wait_bytes(dv_out.at[:, pl.ds(0, away)], sem.at[2])
    wait_own(dq_out.at[:, pl.ds(0, GROUP * HEAD_SIZE)], own.at[0])
    wait_own(dk_out.at[:, pl.ds(0, HEAD_SIZE)], own.at[1])
    wait_own(dv_out.at[:, pl.ds(0, HEAD_SIZE)], own.at[2])


def attend(seq, order, inverse, q_all, k_all, v_all, g_all):
    tokens = k_all.shape[0]
    rows = tokens // seq
    span = tokens // order.shape[0]
    smem = pl.BlockSpec(memory_space=pltpu.SMEM)
    vmem = pl.BlockSpec(memory_space=pltpu.VMEM)
    hbm = pl.BlockSpec(memory_space=pl.ANY)
    table = jnp.asarray(rotary_table(tokens))
    low = jnp.bfloat16
    thin = (tokens, HEAD_SIZE)
    tall = (tokens, BLOCK)
    return pl.pallas_call(
        functools.partial(attend_kernel, seq, span),
        out_shape=(
            jax.ShapeDtypeStruct((rows, seq * GROUP * HEAD_SIZE), low),
            jax.ShapeDtypeStruct((rows, seq * HEAD_SIZE), low),
            jax.ShapeDtypeStruct((rows, seq * HEAD_SIZE), low),
        ),
        in_specs=[smem, smem] + [vmem] * 5,
        out_specs=(hbm,) * 3,
        scratch_shapes=[
            pltpu.VMEM(thin, jnp.float32),
            pltpu.VMEM(thin, jnp.float32),
            pltpu.VMEM((UNIT,) + thin, low),
            pltpu.VMEM(thin, low),
            pltpu.VMEM(thin, low),
            pltpu.VMEM((UNIT,) + thin, low),
            pltpu.VMEM((HEAD_SIZE, tokens), low),
            pltpu.VMEM(thin, jnp.float32),
            pltpu.VMEM(thin, jnp.float32),
            pltpu.VMEM((2, UNIT) + tall, jnp.float32),
            pltpu.VMEM((2, UNIT) + tall, jnp.float32),
            pltpu.VMEM((UNIT, tokens // span, span, HEAD_SIZE), low),
            pltpu.VMEM((tokens // span, span, HEAD_SIZE), low),
            pltpu.VMEM((GROUP,) + thin, low),
            pltpu.VMEM(thin, low),
            pltpu.VMEM(thin, low),
            pltpu.SemaphoreType.DMA((3,)),
            pltpu.SemaphoreType.DMA((3,)),
            pltpu.SemaphoreType.DMA((3,)),
        ],
        compiler_params=pltpu.CompilerParams(
            collective_id=0, has_side_effects=True, vmem_limit_bytes=25 << 20
        ),
        name="attend",
    )(order, inverse, *(
        a.reshape(a.shape[:-2] + (-1, span, a.shape[-1])) for a in (q_all, k_all, v_all, g_all)
    ), table)


def body(sections, seq, q, k, v, g, partner, order):
    span_index = jnp.arange(order.shape[0], dtype=jnp.int32)
    inverse = jnp.sum(
        jnp.where(order[:, None] == span_index[None, :], span_index[:, None], 0), axis=0
    )
    branches = [functools.partial(gather, pair, seq) for pair in range(1, sections)]
    moved = lax.switch(partner[0] - 1, branches, q[0, 0], k[0, 0], v[0, 0], g[0, 0])
    results = attend(seq, order, inverse, *moved)
    return tuple(result[None, None] for result in results)


def solution(mesh):
    placed = P("section", None, "seq", None)
    return jax.shard_map(
        functools.partial(body, mesh.shape["section"], mesh.shape["seq"]),
        mesh=mesh,
        in_specs=(placed, placed, placed, placed, P(), P()),
        out_specs=(placed, placed, placed),
        check_vma=False,
    )
```

time: 195 us -> 160 us (0.82)
  Pallas kernels: 186 us -> 155 us
  local copies, waits for them, and re-layouts: 5.43 us -> 3.17 us
    pallas_call x1, Pallas kernels: 77.6 us -> 59.4 us  [attend(): pl.pallas_call(functools.partial(attend_kernel, seq, span), out_shape=(ja...]
    pallas_call x1, Pallas kernels: 108 us -> 95.9 us  [gather(): pl.pallas_call(functools.partial(gather_kernel, pair, seq), out_shape=(wi...]
    unnamed x9 -> x7, local copies, waits for them, and re-layouts: 5.43 us -> 3.17 us
where the time goes in v2:
time: 160 us
  Pallas kernels  155 us (97%)
  local copies, waits for them, and re-layouts  3.17 us (2%)
    pallas_call x1, Pallas kernels, gather(): pl.pallas_call(functools.partial(gather_kernel, pair, seq), out_shape=(wi...  95.9 us
    pallas_call x1, Pallas kernels, attend(): pl.pallas_call(functools.partial(attend_kernel, seq, span), out_shape=(ja...  59.4 us

profile of v2, /device:TPU:72, one launch (start us, length us, event | category | flops | bytes accessed | tf_op | source)
XLA Modules:
  0.0 160.1 jit_solution(9199200803725031700)
XLA Ops:
  1.3 0.0 copy-start.1
  1.3 0.0 copy-start
  1.3 96.1 %conditional.1 = (bf16[8,16,96,128]{3,2,1,0:T(8,128)(2,1)}, bf16[16,96,128]{2,1,0:T(8,128)(2,1)S(1)}, bf16[16,96,128]{2,1,0:T(8,128)(2,1)S(1)}, bf16[8,16,96,128]{3,2,1,0:T(8,128)(2,1)}) conditional(s32[]{:T(128)} %bitcast.60, (bf16[192,8192]{1,0:T(8,128)(2,1)}, bf16[192,1024]{1,0:T(8,128)(2,1)}, ...), branch_computations={%region_1.2_spmd, %region_2.3_spmd, %region_3.4_spmd, %region_4.5_... | conditional | bytes 32 | solution.py:395
  1.4 95.9 %gather_14.1 = (bf16[8,1536,128]{2,1,0:T(8,128)(2,1)}, bf16[1536,128]{1,0:T(8,128)(2,1)S(1)}, bf16[1536,128]{1,0:T(8,128)(2,1)S(1)}, bf16[8,1536,128]{2,1,0:T(8,128)(2,1)}) custom-call(bf16[192,8192]{1,0:T(8,128)(2,1)} %get-tuple-element.288.q_ref, bf16[192,1024]{1,0:T(8,128)(2,1)} %get-tuple-element.289.k_ref, bf16[192,1024]{1,0:T(8,128)(2,1)} %get-tuple-element.290.v_ref, ...), custom_call_target="tpu_custom_call" | custom-call | tf_op jit(solution)/shard_map/cond/branch_13_fun/gather_14/pallas_call | solution.py:118
  97.4 0.0 copy-done.1
  97.4 0.1 select_reduce_fusion.inverse
  97.5 0.0 copy-done
  97.5 59.4 %attend.1 = (bf16[192,8192]{1,0:T(8,128)(2,1)S(1)}, bf16[192,1024]{1,0:T(8,128)(2,1)S(1)}, bf16[192,1024]{1,0:T(8,128)(2,1)S(1)}) custom-call(s32[16]{0:T(128)S(1)} %copy-done.1, s32[16]{0:T(128)S(1)} %select_reduce_fusion.inverse, bf16[8,16,96,128]{3,2,1,0:T(8,128)(2,1)} %get-tuple-element.314.q_all, bf16[16,96,128]{2,1,0:T(8,128)(2,1)S(1)} %get-tuple-element.315.k_all, ...), custom_call_target="tpu_custom_call" | custom-call | tf_op jit(solution)/shard_map/attend/pallas_call | solution.py:350
  156.9 1.7 %copy.73 = bf16[1,1,192,8192]{3,2,1,0:T(8,128)(2,1)} copy(bf16[1,1,192,8192]{3,2,1,0:T(8,128)(2,1)S(1)} %bitcast.69) | data formatting | bytes 6291456
  158.6 0.7 copy.74
  159.3 0.7 copy.75
Async XLA Ops:
  1.3 96.1 %copy-start.1 = (s32[16]{0:T(128)S(1)}, s32[16]{0:T(128)}, u32[]{:S(2)}) copy-start(s32[16]{0:T(128)} %order.1) | copy-start | bytes 196
  1.3 96.2 %copy-start = (f32[1536,128]{1,0:T(8,128)S(1)}, f32[1536,128]{1,0:T(8,128)}, u32[]{:S(2)}) copy-start(f32[1536,128]{1,0:T(8,128)} %constant.13.clone.table) | copy-start | bytes 2359300
